TPU v7x, 512 devices: a whole 4x8x8 slice. The times are simulated.
512 devices in a mesh: wide: 128 (over y, z, core), narrow: 4 (over x).
Axes of the slice: x: 4, y: 8, z: 8, core: 2. Of those that a mesh axis runs over, the one named last changes fastest.
Arguments:
- grad_out: bfloat16 [32768, 512], P('wide', 'narrow'), may hold values from -24 to 24
- relu_mask: int32 [32768, 512], P('wide', 'narrow'), may hold values 0 or 1
- features: bfloat16 [32768, 512], P('wide', 'narrow'), may hold values from -6 to 6
- hop1_mean: bfloat16 [32768, 512], P('wide', 'narrow'), may hold values from -6 to 6
- hop2_mean: bfloat16 [32768, 512], P('wide', 'narrow'), may hold values from -6 to 6
- w_self: bfloat16 [512, 512], P('narrow'), may hold values from -0.25 to 0.25
- w_hop1: bfloat16 [512, 512], P('narrow'), may hold values from -0.25 to 0.25
- w_hop2: bfloat16 [512, 512], P('narrow'), may hold values from -0.25 to 0.25
- norm: float32 [32768], P('wide'), may hold values from 0.05 to 1
- tile_src: int32 [16384], P('wide'), may hold values from 0 to 1
- tile_owner: int32 [16384], P('wide'), may hold values from 0 to 127, as said below
- tile_block: int32 [16384], P('wide'), may hold values from 0 to 1
- tile_cols: int32 [16384, 128, 8], P('wide'), may hold values from 0 to 127
Outputs:
- grad_features: bfloat16 [32768, 512], P('wide', 'narrow')
- weight_grads: float32 [3, 512, 512], P(None, 'wide', 'narrow')
Inputs may be any that keep to these rules, and one draw needn't show every extreme that they name: `tile_owner`: the 128 tiles of one device name every device once as owner.
All inputs are finite; a program needn't handle non-finite values. No bound on the sum of `relu_mask` on one device may be relied on, other than what follows from the above.
Results may differ from a plain program's by a relative error of at most 0.0054.
Values may be sent and summed in bfloat16 or wider, within the bound.
No kernel may reach another device: no remote copies, remote signals or barrier semaphores. Data moves between devices by JAX's collectives and lax.ppermute only.
A program may use at most 64 MiB of HBM per device.

v0:
```python
import jax
import jax.numpy as jnp
from jax import lax
from jax.sharding import PartitionSpec as P


def tile_pattern(tile_cols):
    positions = jnp.arange(tile_cols.shape[1], dtype=jnp.int32)
    summed = jnp.zeros(tile_cols.shape[:2] + (tile_cols.shape[1],), jnp.int32)
    for column in range(tile_cols.shape[2]):
        summed = summed + (tile_cols[:, :, column, None] == positions).astype(jnp.int32)
    return summed.astype(jnp.bfloat16)


def on_device(
    grad_out,
    relu_mask,
    features,
    hop1_mean,
    hop2_mean,
    w_self,
    w_hop1,
    w_hop2,
    norm,
    tile_src,
    tile_owner,
    tile_block,
    tile_cols,
):
    node_count = features.shape[0]
    local_width = features.shape[1]
    block_rows = tile_cols.shape[1]
    row_blocks = node_count // block_rows
    owner_count = lax.axis_size("wide")
    gated = grad_out * relu_mask.astype(jnp.bfloat16)
    gated_full = lax.all_gather(gated, "narrow", axis=1, tiled=True)
    row_scale = norm[:, None]
    slot_ids = jnp.full((owner_count, 1), -1.0, jnp.float32)
    slot_ids = slot_ids.at[tile_owner, 0].set(tile_block.astype(jnp.float32)).astype(jnp.bfloat16)
    block_marks = jnp.arange(row_blocks, dtype=jnp.float32).astype(jnp.bfloat16)

    def combine_arrived(arrived, arrived_ids):
        select = (arrived_ids[:, 0][None, :] == block_marks[:, None]).astype(jnp.bfloat16)
        summed = jnp.einsum("bs,sjd->bjd", select, arrived, preferred_element_type=jnp.float32)
        return summed.reshape(node_count, local_width)

    pattern = tile_pattern(tile_cols)

    def transpose_hop(scaled):
        picked = scaled.reshape(row_blocks, block_rows, local_width)[tile_src]
        products = jnp.einsum(
            "trj,trd->tjd", pattern, picked, preferred_element_type=jnp.float32
        ).astype(jnp.bfloat16)
        outgoing = (
            jnp.zeros((owner_count, block_rows, local_width), jnp.bfloat16)
            .at[tile_owner]
            .set(products)
        )
        arrived, arrived_ids = (
            lax.all_to_all(outgoing, "wide", split_axis=0, concat_axis=0, tiled=True),
            lax.all_to_all(slot_ids, "wide", split_axis=0, concat_axis=0, tiled=True),
        )
        return combine_arrived(arrived, arrived_ids)

    def project(weight):
        return lax.dot_general(
            gated_full, weight, (((1,), (1,)), ((), ())), preferred_element_type=jnp.float32
        )

    scaled2 = (row_scale * project(w_hop2)).astype(jnp.bfloat16)
    agg2 = transpose_hop(scaled2)
    scaled1 = (row_scale * (project(w_hop1) + agg2)).astype(jnp.bfloat16)
    agg1 = transpose_hop(scaled1)
    grad_features = (project(w_self) + agg1).astype(jnp.bfloat16)
    partial_grads = jnp.stack(
        [
            jnp.einsum("ro,rd->od", gated_full, operand, preferred_element_type=jnp.float32)
            for operand in (features, hop1_mean, hop2_mean)
        ]
    )
    weight_grads = lax.psum_scatter(partial_grads, "wide", scatter_dimension=1, tiled=True)
    return (grad_features, weight_grads)


def solution(mesh):
    placed = (
        P("wide", "narrow"),
        P("wide", "narrow"),
        P("wide", "narrow"),
        P("wide", "narrow"),
        P("wide", "narrow"),
        P("narrow", None),
        P("narrow", None),
        P("narrow", None),
        P("wide"),
        P("wide"),
        P("wide"),
        P("wide"),
        P("wide", None, None),
    )
    return jax.shard_map(
        on_device,
        mesh=mesh,
        in_specs=placed,
        out_specs=(P("wide", "narrow"), P(None, "wide", "narrow")),
        check_vma=False,
    )
```

profile of v0, /device:TPU:24, one launch (start us, length us, event | category | flops | bytes accessed | tf_op | source)
XLA Modules:
  0.0 538.8 jit_solution(16396398977169809282)
XLA Ops:
  7.2 0.0 copy-start
  7.2 0.7 compare_select_fusion.1
  7.9 0.7 convert_element_type.61
  8.5 1.0 scatter_custom_fusion
  9.5 0.8 copy.26
  10.3 17.3 %all-to-all-start = ((bf16[128,1,1]{2,1,0:T(2,128)(2,1)}), bf16[128,1,1]{2,1,0:T(2,128)(2,1)S(1)}, u32[]{:S(2)}, u32[]{:S(2)}) async-start(bf16[128,1,1]{2,1,0:T(2,128)(2,1)} %copy.26), calls=%async_computation | async-start | bytes 131072 | tf_op jit(solution)/shard_map/all_to_all | solution.py:61
  27.6 3.4 fusion.18
  31.1 1.0 convert_multiply_fusion
  32.0 11.9 %all_gather.3 = bf16[256,512]{1,0:T(8,128)(2,1)S(1)} all-gather(bf16[256,128]{1,0:T(8,128)(2,1)S(1)} %convert_multiply_fusion), channel_id=1, replica_groups=mesh['wide'=128,'narrow'=4] {'narrow'}, dimensions={1}, use_global_device_ids=true | all-gather | bytes 327680 | tf_op jit(solution)/shard_map/all_gather | solution.py:36
  44.0 0.7 compare_select_fusion
  44.6 0.0 copy-done
  44.6 0.9 fusion.7
  45.6 3.1 gather_fusion
  48.6 12.0 %convolution_convert_fusion.1 = bf16[128,128,128]{2,1,0:T(8,128)(2,1)} fusion(bf16[128,128,128]{2,1,0:T(8,128)(2,1)} %gather_fusion, s32[128,128]{1,0:T(8,128)S(1)} %bitcast.58, s32[128,128]{1,0:T(8,128)S(1)} %bitcast.60, s32[128,128]{1,0:T(8,128)S(1)} %bitcast.48, s32[128,128]{1,0:T(8,128)S(1)} %bitcast.50, s32[128,128]{1,0:T(8,128)S(1)} %bitcast.52, ...), kind=kOutput, calls=%fused_computation.19 | convolution fusion | flops 589299712 | bytes 8912896 | tf_op jit(solution)/shard_map/trj,trd->tjd/dot_general | solution.py:51
  60.6 3.0 broadcast.17.clone
  63.7 19.4 %scatter_fusion = bf16[128,128,128]{2,1,0:T(8,128)(2,1)} fusion(bf16[128,128,128]{2,1,0:T(8,128)(2,1)} %broadcast.17.clone, s32[128]{0:T(128)S(1)} %compare_select_fusion.1, bf16[128,128,128]{2,1,0:T(8,128)(2,1)} %convolution_convert_fusion.1), kind=kCustom, calls=%fused_computation.3 | custom fusion | bytes 12583424 | tf_op jit(solution)/shard_map/scatter | solution.py:57
  83.0 0.0 all-to-all-done
  83.0 14.2 %all-to-all-start.1 = ((bf16[128,128,128]{2,1,0:T(8,128)(2,1)}), bf16[128,128,128]{2,1,0:T(8,128)(2,1)}, u32[]{:S(2)}, u32[]{:S(2)}) async-start(bf16[128,128,128]{2,1,0:T(8,128)(2,1)} %scatter_fusion), calls=%async_computation.1 | async-start | bytes 8388608 | tf_op jit(solution)/shard_map/all_to_all | solution.py:60
  97.2 0.0 copy-start.1
  97.3 0.0 copy-start.6
  97.3 1.0 reduce
  98.3 99.9 %all-to-all-done.1 = bf16[128,128,128]{2,1,0:T(8,128)(2,1)} async-done(((bf16[128,128,128]{2,1,0:T(8,128)(2,1)}), bf16[128,128,128]{2,1,0:T(8,128)(2,1)}, u32[]{:S(2)}, u32[]{:S(2)}) %all-to-all-start.1) | async-done | bytes 4194336 | tf_op jit(solution)/shard_map/all_to_all | solution.py:60
  198.2 4.5 fusion.2
  202.7 0.0 copy-done.1
  202.7 0.0 copy-done.6
  202.7 0.2 fusion.6
  202.9 3.1 gather_fusion.1
  206.0 12.0 %convolution_convert_fusion = bf16[128,128,128]{2,1,0:T(8,128)(2,1)} fusion(bf16[128,128,128]{2,1,0:T(8,128)(2,1)} %gather_fusion.1, s32[128,128]{1,0:T(8,128)S(1)} %bitcast.59, s32[128,128]{1,0:T(8,128)S(1)} %bitcast.61, s32[128,128]{1,0:T(8,128)S(1)} %bitcast.49, s32[128,128]{1,0:T(8,128)S(1)} %bitcast.51, s32[128,128]{1,0:T(8,128)S(1)} %bitcast.53, ...), kind=kOutput, calls=%fused_computation.18 | convolution fusion | flops 589299712 | bytes 8912896 | tf_op jit(solution)/shard_map/trj,trd->tjd/dot_general | solution.py:51
  218.0 3.0 broadcast.17
  221.0 19.4 %scatter_fusion.1 = bf16[128,128,128]{2,1,0:T(8,128)(2,1)} fusion(bf16[128,128,128]{2,1,0:T(8,128)(2,1)} %broadcast.17, s32[128]{0:T(128)S(1)} %compare_select_fusion.1, bf16[128,128,128]{2,1,0:T(8,128)(2,1)} %convolution_convert_fusion), kind=kCustom, calls=%fused_computation.4 | custom fusion | bytes 12583424 | tf_op jit(solution)/shard_map/scatter | solution.py:57
  240.4 11.5 %all-to-all-start.2 = ((bf16[128,128,128]{2,1,0:T(8,128)(2,1)}), bf16[128,128,128]{2,1,0:T(8,128)(2,1)}, u32[]{:S(2)}, u32[]{:S(2)}) async-start(bf16[128,128,128]{2,1,0:T(8,128)(2,1)} %scatter_fusion.1), calls=%async_computation.2 | async-start | bytes 8388608 | tf_op jit(solution)/shard_map/all_to_all | solution.py:60
  251.9 0.3 all-reduce.4.cloned.1.call-start
  252.2 0.0 copy-done.3
  252.2 0.3 convolution_bitcast_fusion
  252.4 0.0 copy-done.4
  252.4 0.0 copy-start.2
  252.4 0.3 convolution_bitcast_fusion.1
  252.7 0.0 copy-done.5
  252.7 0.3 convolution_bitcast_fusion.2
  253.0 0.9 pad_maximum_fusion
  253.9 0.0 all-reduce.4.cloned.1.call-update
  253.9 1.3 dynamic-slice
  255.9 269.4 %all-reduce.4.cloned.1.call-done = f32[3,512,128]{2,1,0:T(8,128)} async-done(((f32[3,512,128]{2,1,0:T(8,128)}), f32[3,512,128]{2,1,0:T(8,128)}) %all-reduce.4.cloned.1.call-update) | async-done | bytes 786448
  525.3 1.3 constant_dynamic-slice_fusion
  526.6 0.0 all-to-all-done.2
  526.6 4.5 fusion
  531.1 0.0 copy-done.2
  531.1 0.9 fusion.5
  (8 shorter events, 0.0 us)
Async XLA Ops:
  7.2 37.5 %copy-start = (bf16[128,512]{1,0:T(8,128)(2,1)S(1)}, bf16[128,512]{1,0:T(8,128)(2,1)}, u32[]{:S(2)}) copy-start(bf16[128,512]{1,0:T(8,128)(2,1)} %param.20) | copy-start | bytes 393220
  10.3 72.7 %all-to-all-start = ((bf16[128,1,1]{2,1,0:T(2,128)(2,1)}), bf16[128,1,1]{2,1,0:T(2,128)(2,1)S(1)}, u32[]{:S(2)}, u32[]{:S(2)}) async-start(bf16[128,1,1]{2,1,0:T(2,128)(2,1)} %copy.26), calls=%async_computation | async-start | bytes 131072 | tf_op jit(solution)/shard_map/all_to_all | solution.py:61
  83.0 115.1 %all-to-all-start.1 = ((bf16[128,128,128]{2,1,0:T(8,128)(2,1)}), bf16[128,128,128]{2,1,0:T(8,128)(2,1)}, u32[]{:S(2)}, u32[]{:S(2)}) async-start(bf16[128,128,128]{2,1,0:T(8,128)(2,1)} %scatter_fusion), calls=%async_computation.1 | async-start | bytes 8388608 | tf_op jit(solution)/shard_map/all_to_all | solution.py:60
  97.2 105.4 %copy-start.1 = (bf16[128,512]{1,0:T(8,128)(2,1)S(1)}, bf16[128,512]{1,0:T(8,128)(2,1)}, u32[]{:S(2)}) copy-start(bf16[128,512]{1,0:T(8,128)(2,1)} %param.19) | copy-start | bytes 393220
  97.3 105.4 %copy-start.6 = (f32[256]{0:T(256)S(1)}, f32[256]{0:T(256)}, u32[]{:S(2)}) copy-start(f32[256]{0:T(256)} %param.21) | copy-start | bytes 3076
  240.4 11.8 %copy-start.3 = (bf16[256,128]{1,0:T(8,128)(2,1)S(1)}, bf16[256,128]{1,0:T(8,128)(2,1)}, u32[]{:S(2)}) copy-start(bf16[256,128]{1,0:T(8,128)(2,1)} %param.17) | copy-start | bytes 196612
  240.4 12.1 %copy-start.4 = (bf16[256,128]{1,0:T(8,128)(2,1)S(1)}, bf16[256,128]{1,0:T(8,128)(2,1)}, u32[]{:S(2)}) copy-start(bf16[256,128]{1,0:T(8,128)(2,1)} %param.16) | copy-start | bytes 196612
  240.4 12.3 %copy-start.5 = (bf16[256,128]{1,0:T(8,128)(2,1)S(1)}, bf16[256,128]{1,0:T(8,128)(2,1)}, u32[]{:S(2)}) copy-start(bf16[256,128]{1,0:T(8,128)(2,1)} %param.15) | copy-start | bytes 196612
  240.4 286.2 %all-to-all-start.2 = ((bf16[128,128,128]{2,1,0:T(8,128)(2,1)}), bf16[128,128,128]{2,1,0:T(8,128)(2,1)}, u32[]{:S(2)}, u32[]{:S(2)}) async-start(bf16[128,128,128]{2,1,0:T(8,128)(2,1)} %scatter_fusion.1), calls=%async_computation.2 | async-start | bytes 8388608 | tf_op jit(solution)/shard_map/all_to_all | solution.py:60
  251.9 273.4 %all-reduce.4.cloned.1.call-start = ((), (), s32[]{:S(2)}) async-start(), calls=%async_computation.3 | async-start | bytes 1572864
  252.4 278.7 %copy-start.2 = (bf16[128,512]{1,0:T(8,128)(2,1)S(1)}, bf16[128,512]{1,0:T(8,128)(2,1)}, u32[]{:S(2)}) copy-start(bf16[128,512]{1,0:T(8,128)(2,1)} %param.18) | copy-start | bytes 393220
Sparse Core Ops, SparseCore 0:
  255.9 269.2 all-reduce.3
where the time goes:
time: 540 us; the launch traced here: 539 us
  waiting for transfers between devices  369 us (68%)
  local copies, waits for them, and re-layouts  58.7 us (11%)
  starting transfers between devices  43.3 us (8%)
  matrix products  35.8 us (7%)
  between operations  14.9 us (3%)
  blocking collectives  11.9 us (2%)
    unnamed x2, waiting for transfers between devices  269 us
    all_to_all x2, waiting for transfers between devices, transpose_hop(): lax.all_to_all(outgoing, 'wide', split_axis=0, concat_axis=0, tiled=True)  99.9 us
    scatter x2, local copies, waits for them, and re-layouts, transpose_hop(): outgoing = jnp.zeros((owner_count, block_rows, local_width), jnp.bfloat16...  38.7 us
    all_to_all x2, starting transfers between devices, transpose_hop(): lax.all_to_all(outgoing, 'wide', split_axis=0, concat_axis=0, tiled=True)  25.7 us
    dot_general x2, matrix products, transpose_hop(): jnp.einsum('trj,trd->tjd', pattern, picked, preferred_element_type=jnp.fl...  24 us
    all_to_all x1, starting transfers between devices, transpose_hop(): lax.all_to_all(slot_ids, 'wide', split_axis=0, concat_axis=0, tiled=True)  17.3 us
    all_gather x1, blocking collectives, on_device(): gated_full = lax.all_gather(gated, 'narrow', axis=1, tiled=True)  11.9 us
  transfers between devices with their start and end apart: 4, of which 2 were waited for; matrix products, arithmetic and copies ran while one was open for 9% of the time, Pallas kernels for 0%

commit v1 on v0

--- a/solution.py
+++ b/solution.py
@@ -33,7 +33,9 @@
     row_blocks = node_count // block_rows
     owner_count = lax.axis_size("wide")
     gated = grad_out * relu_mask.astype(jnp.bfloat16)
-    gated_full = lax.all_gather(gated, "narrow", axis=1, tiled=True)
+    gated_full = jnp.concatenate(
+        lax.all_to_all(jnp.stack([gated] * lax.axis_size("narrow")), "narrow", 0, 0), axis=1
+    )
     row_scale = norm[:, None]
     slot_ids = jnp.full((owner_count, 1), -1.0, jnp.float32)
     slot_ids = slot_ids.at[tile_owner, 0].set(tile_block.astype(jnp.float32)).astype(jnp.bfloat16)

time: 540 us -> 534 us (0.989)
  blocking collectives: 11.9 us -> 0 us
    all_gather x1 -> x0, blocking collectives: 11.9 us -> none  [on_device(): gated_full = lax.all_gather(gated, 'narrow', axis=1, tiled=True)]
  transfers between devices with their start and end apart: 4 -> 5, of which waited for: 2 -> 2; matrix products, arithmetic and copies ran while one was open for 9% -> 10% of each run, Pallas kernels for 0% -> 0%
where the time goes in v1:
time: 534 us; the launch traced here: 533 us
  waiting for transfers between devices  370 us (69%)
  local copies, waits for them, and re-layouts  59.5 us (11%)
  starting transfers between devices  47.7 us (9%)
  matrix products  35.8 us (7%)
  between operations  14.9 us (3%)
    unnamed x2, waiting for transfers between devices  270 us
    all_to_all x2, waiting for transfers between devices, transpose_hop(): lax.all_to_all(outgoing, 'wide', split_axis=0, concat_axis=0, tiled=True)  99.9 us
    scatter x2, local copies, waits for them, and re-layouts, transpose_hop(): outgoing = jnp.zeros((owner_count, block_rows, local_width), jnp.bfloat16...  38.7 us
    all_to_all x2, starting transfers between devices, transpose_hop(): lax.all_to_all(outgoing, 'wide', split_axis=0, concat_axis=0, tiled=True)  25.8 us
    dot_general x2, matrix products, transpose_hop(): jnp.einsum('trj,trd->tjd', pattern, picked, preferred_element_type=jnp.fl...  24 us
    all_to_all x1, starting transfers between devices, transpose_hop(): lax.all_to_all(slot_ids, 'wide', split_axis=0, concat_axis=0, tiled=True)  17.4 us
  transfers between devices with their start and end apart: 5, of which 2 were waited for; matrix products, arithmetic and copies ran while one was open for 10% of the time, Pallas kernels for 0%

profile of v1, /device:TPU:24, one launch (start us, length us, event | category | flops | bytes accessed | tf_op | source)
XLA Modules:
  0.0 532.9 jit_solution(2614324023005099750)
XLA Ops:
  7.2 0.0 copy-start
  7.2 1.0 convert_multiply_fusion
  8.2 0.1 copy.28
  8.3 0.7 stack.19
  9.0 4.3 all-to-all-start
  13.3 0.7 compare_select_fusion
  14.0 0.7 compare_select_fusion.1
  14.6 0.7 convert_element_type.61
  15.3 1.0 scatter_custom_fusion
  16.3 0.8 copy.29
  17.0 3.4 fusion.18
  20.5 0.0 all-to-all-done
  20.5 17.4 %all-to-all-start.1 = ((bf16[128,1,1]{2,1,0:T(2,128)(2,1)}), bf16[128,1,1]{2,1,0:T(2,128)(2,1)S(1)}, u32[]{:S(2)}, u32[]{:S(2)}) async-start(bf16[128,1,1]{2,1,0:T(2,128)(2,1)} %copy.29), calls=%async_computation.1 | async-start | bytes 131072 | tf_op jit(solution)/shard_map/all_to_all | solution.py:63
  37.8 0.0 copy-done
  37.8 0.9 fusion.7
  38.8 3.1 gather_fusion
  41.9 12.0 %convolution_convert_fusion.1 = bf16[128,128,128]{2,1,0:T(8,128)(2,1)} fusion(bf16[128,128,128]{2,1,0:T(8,128)(2,1)} %gather_fusion, s32[128,128]{1,0:T(8,128)S(1)} %bitcast.67, s32[128,128]{1,0:T(8,128)S(1)} %bitcast.69, s32[128,128]{1,0:T(8,128)S(1)} %bitcast.57, s32[128,128]{1,0:T(8,128)S(1)} %bitcast.59, s32[128,128]{1,0:T(8,128)S(1)} %bitcast.61, ...), kind=kOutput, calls=%fused_computation.19 | convolution fusion | flops 589299712 | bytes 8912896 | tf_op jit(solution)/shard_map/trj,trd->tjd/dot_general | solution.py:53
  53.9 3.0 broadcast.19.clone
  56.9 19.3 %scatter_fusion = bf16[128,128,128]{2,1,0:T(8,128)(2,1)} fusion(bf16[128,128,128]{2,1,0:T(8,128)(2,1)} %broadcast.19.clone, s32[128]{0:T(128)S(1)} %compare_select_fusion.1, bf16[128,128,128]{2,1,0:T(8,128)(2,1)} %convolution_convert_fusion.1), kind=kCustom, calls=%fused_computation.3 | custom fusion | bytes 12583424 | tf_op jit(solution)/shard_map/scatter | solution.py:59
  76.2 0.0 all-to-all-done.1
  76.2 14.2 %all-to-all-start.2 = ((bf16[128,128,128]{2,1,0:T(8,128)(2,1)}), bf16[128,128,128]{2,1,0:T(8,128)(2,1)}, u32[]{:S(2)}, u32[]{:S(2)}) async-start(bf16[128,128,128]{2,1,0:T(8,128)(2,1)} %scatter_fusion), calls=%async_computation.2 | async-start | bytes 8388608 | tf_op jit(solution)/shard_map/all_to_all | solution.py:62
  90.5 0.0 copy-start.1
  90.5 0.0 copy-start.6
  90.5 1.0 reduce
  91.5 99.9 %all-to-all-done.2 = bf16[128,128,128]{2,1,0:T(8,128)(2,1)} async-done(((bf16[128,128,128]{2,1,0:T(8,128)(2,1)}), bf16[128,128,128]{2,1,0:T(8,128)(2,1)}, u32[]{:S(2)}, u32[]{:S(2)}) %all-to-all-start.2) | async-done | bytes 4194336 | tf_op jit(solution)/shard_map/all_to_all | solution.py:62
  191.4 4.5 fusion.2
  195.9 0.0 copy-done.1
  195.9 0.0 copy-done.6
  195.9 0.3 fusion.6
  196.2 3.1 gather_fusion.1
  199.3 12.0 %convolution_convert_fusion = bf16[128,128,128]{2,1,0:T(8,128)(2,1)} fusion(bf16[128,128,128]{2,1,0:T(8,128)(2,1)} %gather_fusion.1, s32[128,128]{1,0:T(8,128)S(1)} %bitcast.68, s32[128,128]{1,0:T(8,128)S(1)} %bitcast.70, s32[128,128]{1,0:T(8,128)S(1)} %bitcast.58, s32[128,128]{1,0:T(8,128)S(1)} %bitcast.60, s32[128,128]{1,0:T(8,128)S(1)} %bitcast.62, ...), kind=kOutput, calls=%fused_computation.18 | convolution fusion | flops 589299712 | bytes 8912896 | tf_op jit(solution)/shard_map/trj,trd->tjd/dot_general | solution.py:53
  211.3 3.0 broadcast.19
  214.3 19.3 %scatter_fusion.1 = bf16[128,128,128]{2,1,0:T(8,128)(2,1)} fusion(bf16[128,128,128]{2,1,0:T(8,128)(2,1)} %broadcast.19, s32[128]{0:T(128)S(1)} %compare_select_fusion.1, bf16[128,128,128]{2,1,0:T(8,128)(2,1)} %convolution_convert_fusion), kind=kCustom, calls=%fused_computation.4 | custom fusion | bytes 12583424 | tf_op jit(solution)/shard_map/scatter | solution.py:59
  233.6 11.6 %all-to-all-start.3 = ((bf16[128,128,128]{2,1,0:T(8,128)(2,1)}), bf16[128,128,128]{2,1,0:T(8,128)(2,1)}, u32[]{:S(2)}, u32[]{:S(2)}) async-start(bf16[128,128,128]{2,1,0:T(8,128)(2,1)} %scatter_fusion.1), calls=%async_computation.3 | async-start | bytes 8388608 | tf_op jit(solution)/shard_map/all_to_all | solution.py:62
  245.2 0.3 all-reduce.4.cloned.1.call-start
  245.5 0.2 convolution_bitcast_fusion
  245.7 0.0 copy-start.2
  245.7 0.2 convolution_bitcast_fusion.1
  246.0 0.2 convolution_bitcast_fusion.2
  246.2 0.9 pad_maximum_fusion
  247.1 0.0 all-reduce.4.cloned.1.call-update
  247.1 1.3 dynamic-slice
  249.1 270.2 %all-reduce.4.cloned.1.call-done = f32[3,512,128]{2,1,0:T(8,128)} async-done(((f32[3,512,128]{2,1,0:T(8,128)}), f32[3,512,128]{2,1,0:T(8,128)}) %all-reduce.4.cloned.1.call-update) | async-done | bytes 786448
  519.3 1.3 constant_dynamic-slice_fusion
  520.6 0.0 all-to-all-done.3
  520.6 4.5 fusion
  525.1 0.0 copy-done.2
  525.1 0.9 fusion.5
  (11 shorter events, 0.0 us)
Async XLA Ops:
  7.2 30.7 %copy-start = (bf16[128,512]{1,0:T(8,128)(2,1)S(1)}, bf16[128,512]{1,0:T(8,128)(2,1)}, u32[]{:S(2)}) copy-start(bf16[128,512]{1,0:T(8,128)(2,1)} %param.20) | copy-start | bytes 393220
  9.0 11.5 %all-to-all-start = ((bf16[4,256,128]{1,2,0:T(8,128)(2,1)}), bf16[4,256,128]{1,2,0:T(8,128)(2,1)S(1)}, u32[]{:S(2)}, u32[]{:S(2)}) async-start(bf16[4,256,128]{1,2,0:T(8,128)(2,1)} %stack.19), calls=%async_computation | async-start | bytes 524288 | tf_op jit(solution)/shard_map/all_to_all | solution.py:37
  20.5 55.8 %all-to-all-start.1 = ((bf16[128,1,1]{2,1,0:T(2,128)(2,1)}), bf16[128,1,1]{2,1,0:T(2,128)(2,1)S(1)}, u32[]{:S(2)}, u32[]{:S(2)}) async-start(bf16[128,1,1]{2,1,0:T(2,128)(2,1)} %copy.29), calls=%async_computation.1 | async-start | bytes 131072 | tf_op jit(solution)/shard_map/all_to_all | solution.py:63
  76.2 115.1 %all-to-all-start.2 = ((bf16[128,128,128]{2,1,0:T(8,128)(2,1)}), bf16[128,128,128]{2,1,0:T(8,128)(2,1)}, u32[]{:S(2)}, u32[]{:S(2)}) async-start(bf16[128,128,128]{2,1,0:T(8,128)(2,1)} %scatter_fusion), calls=%async_computation.2 | async-start | bytes 8388608 | tf_op jit(solution)/shard_map/all_to_all | solution.py:62
  90.5 105.4 %copy-start.1 = (bf16[128,512]{1,0:T(8,128)(2,1)S(1)}, bf16[128,512]{1,0:T(8,128)(2,1)}, u32[]{:S(2)}) copy-start(bf16[128,512]{1,0:T(8,128)(2,1)} %param.19) | copy-start | bytes 393220
  90.5 105.4 %copy-start.6 = (f32[256]{0:T(256)S(1)}, f32[256]{0:T(256)}, u32[]{:S(2)}) copy-start(f32[256]{0:T(256)} %param.21) | copy-start | bytes 3076
  233.6 11.8 %copy-start.3 = (bf16[256,128]{1,0:T(8,128)(2,1)S(1)}, bf16[256,128]{1,0:T(8,128)(2,1)}, u32[]{:S(2)}) copy-start(bf16[256,128]{1,0:T(8,128)(2,1)} %param.17) | copy-start | bytes 196612
  233.6 12.1 %copy-start.4 = (bf16[256,128]{1,0:T(8,128)(2,1)S(1)}, bf16[256,128]{1,0:T(8,128)(2,1)}, u32[]{:S(2)}) copy-start(bf16[256,128]{1,0:T(8,128)(2,1)} %param.16) | copy-start | bytes 196612
  233.6 12.3 %copy-start.5 = (bf16[256,128]{1,0:T(8,128)(2,1)S(1)}, bf16[256,128]{1,0:T(8,128)(2,1)}, u32[]{:S(2)}) copy-start(bf16[256,128]{1,0:T(8,128)(2,1)} %param.15) | copy-start | bytes 196612
  233.6 287.0 %all-to-all-start.3 = ((bf16[128,128,128]{2,1,0:T(8,128)(2,1)}), bf16[128,128,128]{2,1,0:T(8,128)(2,1)}, u32[]{:S(2)}, u32[]{:S(2)}) async-start(bf16[128,128,128]{2,1,0:T(8,128)(2,1)} %scatter_fusion.1), calls=%async_computation.3 | async-start | bytes 8388608 | tf_op jit(solution)/shard_map/all_to_all | solution.py:62
  245.2 274.1 %all-reduce.4.cloned.1.call-start = ((), (), s32[]{:S(2)}) async-start(), calls=%async_computation.4 | async-start | bytes 1572864
  245.7 279.4 %copy-start.2 = (bf16[128,512]{1,0:T(8,128)(2,1)S(1)}, bf16[128,512]{1,0:T(8,128)(2,1)}, u32[]{:S(2)}) copy-start(bf16[128,512]{1,0:T(8,128)(2,1)} %param.18) | copy-start | bytes 393220
Sparse Core Ops, SparseCore 0:
  249.2 270.0 all-reduce.3
